TPU v7x, 32 devices: a whole 2x2x4 slice. The times are simulated.
32 devices in a mesh: outer: 4 (over z), dev: 8 (over y, x, core).
Axes of the slice: x: 2, y: 2, z: 4, core: 2. Of those that a mesh axis runs over, the one named last changes fastest.
Arguments:
- partials: bfloat16 [32, 8192, 128], P(('outer', 'dev')), may hold values from -6 to 6
- p_old: bfloat16 [8192, 1024], P('dev'), may hold values from -0.0625 to 0.0625
- p_new: bfloat16 [8192, 1024], P('dev'), may hold values from -0.0625 to 0.0625
- weight: float32 [8192, 128], P('dev'), may hold values from -4 to 4
- m_old: float32 [1024, 128], P('dev'), may hold values from -96 to 96
- v_old: float32 [1024, 128], P('dev'), may hold values from 32 to 1280
Outputs:
- new_weight: float32 [8192, 128], P('dev')
- m_new: float32 [1024, 128], P('dev')
- v_new: float32 [1024, 128], P('dev')
All inputs are finite; a program needn't handle non-finite values.
Results may differ from a plain program's by a relative error of at most 0.0012.
Values may be sent and summed in bfloat16 or wider, within the bound.
A program may use at most 128 MiB of HBM per device.

v0:
```python
import jax
import jax.numpy as jnp
from jax import lax
from jax.sharding import PartitionSpec as P

beta_mean = 0.9
beta_square = 0.95
bias_mean = 0.9999734386011124
bias_square = 0.9940794707796659
adam_epsilon = 1e-08
step_scale = 0.5


def on_device(partials, p_old, p_new, weight, m_old, v_old):
    local_grad = partials[0].astype(jnp.float32)
    grad_rows = lax.psum_scatter(local_grad, "dev", scatter_dimension=0, tiled=True)
    basis = p_new.astype(jnp.float32)
    columns = basis
    projected = lax.psum_scatter(
        jnp.dot(columns.T, grad_rows, precision=lax.Precision.HIGHEST),
        "dev",
        scatter_dimension=0,
        tiled=True,
    )
    projected = lax.psum(projected, "outer")
    columns = p_new
    margin_rows = lax.psum_scatter(
        jnp.dot(columns.T, p_old, preferred_element_type=jnp.float32),
        "dev",
        scatter_dimension=0,
        tiled=True,
    )
    first_piece = lax.all_gather(m_old, "dev", axis=0, tiled=True)
    second_piece = lax.all_gather(v_old, "dev", axis=0, tiled=True)
    first = jnp.dot(margin_rows, first_piece, precision=lax.Precision.HIGHEST)
    second = jnp.dot(margin_rows * margin_rows, second_piece, precision=lax.Precision.HIGHEST)
    m_new = beta_mean * first + (1.0 - beta_mean) * projected
    v_new = beta_square * second + (1.0 - beta_square) * projected * projected
    direction = (m_new / bias_mean / (jnp.sqrt(v_new / bias_square) + adam_epsilon)).astype(
        jnp.bfloat16
    )
    columns = p_new
    update = jnp.dot(
        columns,
        lax.all_gather(direction, "dev", axis=0, tiled=True),
        preferred_element_type=jnp.float32,
    )
    new_weight = weight - step_scale * update
    return (new_weight, m_new, v_new)


def solution(mesh):
    in_specs = (
        P(("outer", "dev"), None, None),
        P("dev", None),
        P("dev", None),
        P("dev", None),
        P("dev", None),
        P("dev", None),
    )
    out_specs = (P("dev", None), P("dev", None), P("dev", None))
    return jax.shard_map(
        on_device, mesh=mesh, in_specs=in_specs, out_specs=out_specs, check_vma=False
    )
```

profile of v0, /device:TPU:0, one launch (start us, length us, event | category | flops | bytes accessed | tf_op | source)
XLA Modules:
  0.0 216.5 jit_solution(17691967801441322931)
XLA Ops:
  7.2 0.0 reduce-scatter.6.cloned.1.call-start
  7.2 3.9 %bitcast_convert_fusion = f32[8192,128]{1,0:T(8,128)} fusion(bf16[1,8192,128]{2,1,0:T(8,128)(2,1)} %param.6), kind=kLoop, calls=%fused_computation | loop fusion | flops 1048576 | bytes 6291456 | tf_op jit(solution)/shard_map/convert_element_type | solution.py:15
  11.2 0.0 reduce-scatter.6.cloned.1.call-update
  11.2 0.0 reduce-scatter.8.cloned.1.call-start
  11.2 54.0 %reduce-scatter.6.cloned.1.call-done = f32[1024,128]{1,0:T(8,128)} async-done(((f32[8192,128]{1,0:T(8,128)}), f32[1024,128]{1,0:T(8,128)}) %reduce-scatter.6.cloned.1.call-update) | async-done | bytes 524304 | tf_op jit(solution)/shard_map/reduce_scatter | solution.py:16
  65.3 4.1 %fusion.6 = f32[1024,128]{1,0:T(8,128)} fusion(bf16[1024,1024]{1,0:T(8,128)(2,1)S(1)} %copy-done, f32[1024,128]{1,0:T(8,128)} %reduce-scatter.6.cloned.1.call-done), kind=kOutput, calls=%fused_computation.12 | convolution fusion | flops 1610612736 | bytes 3145728 | tf_op jit(solution)/shard_map/dot_general | solution.py:20
  69.4 0.0 reduce-scatter.8.cloned.1.call-update
  69.5 0.0 reduce-scatter.4.cloned.1.call-start
  69.5 5.9 %fusion.5 = f32[1024,1024]{1,0:T(8,128)} fusion(bf16[1024,1024]{1,0:T(8,128)(2,1)S(1)} %copy-done, bf16[1024,1024]{1,0:T(8,128)(2,1)} %param.7), kind=kOutput, calls=%fused_computation.11 | convolution fusion | flops 2147483648 | bytes 8388608 | tf_op jit(solution)/shard_map/dot_general | solution.py:28
  75.4 0.0 reduce-scatter.4.cloned.1.call-update
  75.5 0.0 all-reduce.2.cloned.1.call-start
  75.5 1.0 copy-done.2
  76.5 1.0 copy.9
  77.5 9.8 %all_gather.9 = f32[1024,128]{1,0:T(8,128)S(1)} all-gather(f32[128,128]{1,0:T(8,128)S(1)} %copy-done.4), channel_id=1, replica_groups=mesh['outer'=4,'dev'=8] {'dev'}, dimensions={0}, use_global_device_ids=true | all-gather | bytes 589824 | tf_op jit(solution)/shard_map/all_gather | solution.py:33
  87.2 16.5 %reduce-scatter.8.cloned.1.call-done = f32[128,128]{1,0:T(8,128)} async-done(((f32[1024,128]{1,0:T(8,128)}), f32[128,128]{1,0:T(8,128)}) %reduce-scatter.8.cloned.1.call-update) | async-done | bytes 65552 | tf_op jit(solution)/shard_map/reduce_scatter | solution.py:19
  103.7 0.0 all-reduce.2.cloned.1.call-update
  103.8 9.8 %all_gather.10 = f32[1024,128]{1,0:T(8,128)S(1)} all-gather(f32[128,128]{1,0:T(8,128)S(1)} %copy-done.5), channel_id=1, replica_groups=mesh['outer'=4,'dev'=8] {'dev'}, dimensions={0}, use_global_device_ids=true | all-gather | bytes 589824 | tf_op jit(solution)/shard_map/all_gather | solution.py:34
  113.5 44.7 %reduce-scatter.4.cloned.1.call-done = f32[128,1024]{1,0:T(8,128)} async-done(((f32[1024,1024]{1,0:T(8,128)}), f32[128,1024]{1,0:T(8,128)}) %reduce-scatter.4.cloned.1.call-update) | async-done | bytes 524304 | tf_op jit(solution)/shard_map/reduce_scatter | solution.py:27
  158.3 36.5 %all-reduce.2.cloned.1.call-done = f32[128,128]{1,0:T(8,128)} async-done(((f32[128,128]{1,0:T(8,128)}), f32[128,128]{1,0:T(8,128)}) %all-reduce.2.cloned.1.call-update) | async-done | bytes 65552 | tf_op jit(solution)/shard_map/psum | solution.py:25
  194.8 1.7 fusion.3
  196.5 2.4 %divide_convert_fusion = (bf16[128,128]{1,0:T(8,128)(2,1)S(1)}, f32[128,128]{1,0:T(8,128)}) fusion(f32[128,128]{1,0:T(8,128)S(1)} %fusion.3, f32[128,128]{1,0:T(8,128)} %all-reduce.2.cloned.1.call-done, f32[1024,128]{1,0:T(8,128)S(1)} %all_gather.10, f32[128,1024]{1,0:T(8,128)} %reduce-scatter.4.cloned.1.call-done), kind=kOutput, calls=%fused_computation.10 | convolution fusion | flops 201605120 | bytes 1277952 | tf_op jit(solution)/shard_map/dot_general | solution.py:36
  198.9 9.2 %all_gather.11 = bf16[1024,128]{1,0:T(8,128)(2,1)S(1)} all-gather(bf16[128,128]{1,0:T(8,128)(2,1)S(1)} %get-tuple-element.6), channel_id=1, replica_groups=mesh['outer'=4,'dev'=8] {'dev'}, dimensions={0}, use_global_device_ids=true | all-gather | bytes 294912 | tf_op jit(solution)/shard_map/all_gather | solution.py:45
  208.1 0.8 fusion.1
  209.0 1.0 copy.10
  (11 shorter events, 0.0 us)
Async XLA Ops:
  7.2 58.1 %copy-start = (bf16[1024,1024]{1,0:T(8,128)(2,1)S(1)}, bf16[1024,1024]{1,0:T(8,128)(2,1)}, u32[]{:S(2)}) copy-start(bf16[1024,1024]{1,0:T(8,128)(2,1)} %param.8) | copy-start | bytes 6291460
  7.2 58.1 %reduce-scatter.6.cloned.1.call-start = ((), (), s32[]{:S(2)}) async-start(), calls=%async_computation.4 | async-start | bytes 4718592 | tf_op jit(solution)/shard_map/reduce_scatter | solution.py:16
  11.2 92.5 %reduce-scatter.8.cloned.1.call-start = ((), (), s32[]{:S(2)}) async-start(), calls=%async_computation.5 | async-start | bytes 589824 | tf_op jit(solution)/shard_map/reduce_scatter | solution.py:19
  69.5 88.8 %reduce-scatter.4.cloned.1.call-start = ((), (), s32[]{:S(2)}) async-start(), calls=%async_computation.3 | async-start | bytes 4718592 | tf_op jit(solution)/shard_map/reduce_scatter | solution.py:27
  75.4 1.0 copy-start.2
  75.4 2.0 copy-start.4
  75.4 28.3 %copy-start.5 = (f32[128,128]{1,0:T(8,128)S(1)}, f32[128,128]{1,0:T(8,128)}, u32[]{:S(2)}) copy-start(f32[128,128]{1,0:T(8,128)} %param.11) | copy-start | bytes 196612
  75.5 119.3 %all-reduce.2.cloned.1.call-start = ((), (), s32[]{:S(2)}) async-start(), calls=%async_computation.6 | async-start | bytes 131072 | tf_op jit(solution)/shard_map/psum | solution.py:25
  194.8 13.4 %copy-start.1 = (f32[1024,128]{0,1:T(8,128)S(1)}, f32[1024,128]{0,1:T(8,128)}, u32[]{:S(2)}) copy-start(f32[1024,128]{0,1:T(8,128)} %copy.9) | copy-start | bytes 1572868
  196.5 12.5 %copy-start.3 = (f32[128,128]{1,0:T(8,128)}, f32[128,128]{1,0:T(8,128)S(1)}, u32[]{:S(2)}) copy-start(f32[128,128]{1,0:T(8,128)S(1)} %fusion.3) | copy-start | bytes 196612
Sparse Core Ops, SparseCore 0:
  11.3 53.8 reduce-scatter.5
  69.6 34.0 reduce-scatter.7
  107.1 51.1 reduce-scatter.3
  160.5 34.2 all-reduce.1
where the time goes:
time: 217 us
  waiting for transfers between devices  152 us (70%)
  blocking collectives  28.8 us (13%)
  matrix products  15 us (7%)
  between operations  13.8 us (6%)
  other arithmetic  3.94 us (2%)
  local copies, waits for them, and re-layouts  2.99 us (1%)
    reduce_scatter x1, waiting for transfers between devices, on_device(): lax.psum_scatter(local_grad, 'dev', scatter_dimension=0, tiled=True)  54 us
    reduce_scatter x1, waiting for transfers between devices, on_device(): lax.psum_scatter(jnp.dot(columns.T, p_old, preferred_element_type=jnp.flo...  44.7 us
    psum x1, waiting for transfers between devices, on_device(): projected = lax.psum(projected, 'outer')  36.5 us
    reduce_scatter x1, waiting for transfers between devices, on_device(): lax.psum_scatter(jnp.dot(columns.T, grad_rows, precision=lax.Precision.HI...  16.5 us
    all_gather x1, blocking collectives, on_device(): second_piece = lax.all_gather(v_old, 'dev', axis=0, tiled=True)  9.79 us
    all_gather x1, blocking collectives, on_device(): first_piece = lax.all_gather(m_old, 'dev', axis=0, tiled=True)  9.77 us
    all_gather x1, blocking collectives, on_device(): lax.all_gather(direction, 'dev', axis=0, tiled=True)  9.25 us
    dot_general x1, matrix products, on_device(): jnp.dot(columns.T, p_old, preferred_element_type=jnp.float32)  5.92 us
  transfers between devices with their start and end apart: 4, of which 4 were waited for; matrix products, arithmetic and copies ran while one was open for 3% of the time, Pallas kernels for 0%

commit v1 on v0

--- a/solution.py
+++ b/solution.py
@@ -22,7 +22,7 @@
         scatter_dimension=0,
         tiled=True,
     )
-    projected = lax.psum(projected, "outer")
+    projected = jnp.sum(lax.all_gather(projected, "outer"), axis=0)
     columns = p_new
     margin_rows = lax.psum_scatter(
         jnp.dot(columns.T, p_old, preferred_element_type=jnp.float32),

time: 217 us -> 181 us (0.83)
  waiting for transfers between devices: 152 us -> 102 us
  blocking collectives: 28.8 us -> 42.6 us
    psum x1 -> x0, waiting for transfers between devices: 36.5 us -> none  [on_device(): projected = lax.psum(projected, 'outer')]
    all_gather x0 -> x1, blocking collectives: none -> 14 us  [on_device(): projected = jnp.sum(lax.all_gather(projected, 'outer'), axis=0)]
    reduce_scatter x1, waiting for transfers between devices: 16.5 us -> 7.43 us  [on_device(): lax.psum_scatter(jnp.dot(columns.T, grad_rows, precision=lax.Precision.HI...]
    reduce_scatter x1, waiting for transfers between devices: 44.7 us -> 40.5 us  [on_device(): lax.psum_scatter(jnp.dot(columns.T, p_old, preferred_element_type=jnp.flo...]
  transfers between devices with their start and end apart: 4 -> 3, of which waited for: 4 -> 3; matrix products, arithmetic and copies ran while one was open for 3% -> 4% of each run, Pallas kernels for 0% -> 0%
where the time goes in v1:
time: 181 us
  waiting for transfers between devices  102 us (56%)
  blocking collectives  42.6 us (24%)
  matrix products  15 us (8%)
  between operations  13.8 us (8%)
  other arithmetic  3.95 us (2%)
  local copies, waits for them, and re-layouts  3.04 us (2%)
    reduce_scatter x1, waiting for transfers between devices, on_device(): lax.psum_scatter(local_grad, 'dev', scatter_dimension=0, tiled=True)  54.1 us
    reduce_scatter x1, waiting for transfers between devices, on_device(): lax.psum_scatter(jnp.dot(columns.T, p_old, preferred_element_type=jnp.flo...  40.5 us
    all_gather x1, blocking collectives, on_device(): projected = jnp.sum(lax.all_gather(projected, 'outer'), axis=0)  14 us
    all_gather x1, blocking collectives, on_device(): first_piece = lax.all_gather(m_old, 'dev', axis=0, tiled=True)  9.77 us
    all_gather x1, blocking collectives, on_device(): second_piece = lax.all_gather(v_old, 'dev', axis=0, tiled=True)  9.58 us
    all_gather x1, blocking collectives, on_device(): lax.all_gather(direction, 'dev', axis=0, tiled=True)  9.23 us
    reduce_scatter x1, waiting for transfers between devices, on_device(): lax.psum_scatter(jnp.dot(columns.T, grad_rows, precision=lax.Precision.HI...  7.43 us
    dot_general x1, matrix products, on_device(): jnp.dot(columns.T, p_old, preferred_element_type=jnp.float32)  5.91 us
  transfers between devices with their start and end apart: 3, of which 3 were waited for; matrix products, arithmetic and copies ran while one was open for 4% of the time, Pallas kernels for 0%

profile of v1, /device:TPU:0, one launch (start us, length us, event | category | flops | bytes accessed | tf_op | source)
XLA Modules:
  0.0 180.6 jit_solution(1117037717697461161)
XLA Ops:
  7.2 0.0 copy-start
  7.2 0.0 reduce-scatter.6.cloned.1.call-start
  7.2 3.9 %bitcast_convert_fusion = f32[8192,128]{1,0:T(8,128)} fusion(bf16[1,8192,128]{2,1,0:T(8,128)(2,1)} %param.6), kind=kLoop, calls=%fused_computation | loop fusion | flops 1048576 | bytes 6291456 | tf_op jit(solution)/shard_map/convert_element_type | solution.py:15
  11.2 0.0 reduce-scatter.6.cloned.1.call-update
  11.2 0.0 reduce-scatter.8.cloned.1.call-start
  11.2 54.1 %reduce-scatter.6.cloned.1.call-done = f32[1024,128]{1,0:T(8,128)} async-done(((f32[8192,128]{1,0:T(8,128)}), f32[1024,128]{1,0:T(8,128)}) %reduce-scatter.6.cloned.1.call-update) | async-done | bytes 524304 | tf_op jit(solution)/shard_map/reduce_scatter | solution.py:16
  65.3 4.2 %fusion.6 = f32[1024,128]{1,0:T(8,128)} fusion(bf16[1024,1024]{1,0:T(8,128)(2,1)S(1)} %copy-done, f32[1024,128]{1,0:T(8,128)} %reduce-scatter.6.cloned.1.call-done), kind=kOutput, calls=%fused_computation.12 | convolution fusion | flops 1610612736 | bytes 3145728 | tf_op jit(solution)/shard_map/dot_general | solution.py:20
  69.5 0.0 reduce-scatter.8.cloned.1.call-update
  69.5 0.0 reduce-scatter.4.cloned.1.call-start
  69.5 5.9 %fusion.5 = f32[1024,1024]{1,0:T(8,128)} fusion(bf16[1024,1024]{1,0:T(8,128)(2,1)S(1)} %copy-done, bf16[1024,1024]{1,0:T(8,128)(2,1)} %param.7), kind=kOutput, calls=%fused_computation.11 | convolution fusion | flops 2147483648 | bytes 8388608 | tf_op jit(solution)/shard_map/dot_general | solution.py:28
  75.5 0.0 reduce-scatter.4.cloned.1.call-update
  75.5 1.0 copy-done.2
  76.5 1.0 copy.9
  77.5 9.8 %all_gather.15 = f32[1024,128]{1,0:T(8,128)S(1)} all-gather(f32[128,128]{1,0:T(8,128)S(1)} %copy-done.4), channel_id=1, replica_groups=mesh['outer'=4,'dev'=8] {'dev'}, dimensions={0}, use_global_device_ids=true | all-gather | bytes 589824 | tf_op jit(solution)/shard_map/all_gather | solution.py:33
  87.3 9.6 %all_gather.18 = f32[1024,128]{1,0:T(8,128)S(1)} all-gather(f32[128,128]{1,0:T(8,128)S(1)} %copy-done.5), channel_id=1, replica_groups=mesh['outer'=4,'dev'=8] {'dev'}, dimensions={0}, use_global_device_ids=true | all-gather | bytes 589824 | tf_op jit(solution)/shard_map/all_gather | solution.py:34
  96.8 7.4 %reduce-scatter.8.cloned.1.call-done = f32[128,128]{1,0:T(8,128)} async-done(((f32[1024,128]{1,0:T(8,128)}), f32[128,128]{1,0:T(8,128)}) %reduce-scatter.8.cloned.1.call-update) | async-done | bytes 65552 | tf_op jit(solution)/shard_map/reduce_scatter | solution.py:19
  104.3 14.0 %all-gather = f32[512,128]{1,0:T(8,128)S(1)} all-gather(f32[128,128]{1,0:T(8,128)} %reduce-scatter.8.cloned.1.call-done), channel_id=2, replica_groups=mesh['outer'=4,'dev'=8] {'outer'}, dimensions={0}, use_global_device_ids=true | all-gather | bytes 327680 | tf_op jit(solution)/shard_map/all_gather | solution.py:25
  118.3 40.5 %reduce-scatter.4.cloned.1.call-done = f32[128,1024]{1,0:T(8,128)} async-done(((f32[1024,1024]{1,0:T(8,128)}), f32[128,1024]{1,0:T(8,128)}) %reduce-scatter.4.cloned.1.call-update) | async-done | bytes 524304 | tf_op jit(solution)/shard_map/reduce_scatter | solution.py:27
  158.8 1.7 fusion.3
  160.6 0.0 copy-start.3
  160.6 2.4 %divide_convert_fusion = (bf16[128,128]{1,0:T(8,128)(2,1)S(1)}, f32[128,128]{1,0:T(8,128)}) fusion(f32[128,128]{1,0:T(8,128)S(1)} %fusion.3, f32[128,128]{1,0:T(8,128)S(1)} %reduce_sum.9, f32[1024,128]{1,0:T(8,128)S(1)} %all_gather.18, f32[128,1024]{1,0:T(8,128)} %reduce-scatter.4.cloned.1.call-done), kind=kOutput, calls=%fused_computation.10 | convolution fusion | flops 201605120 | bytes 1277952 | tf_op jit(solution)/shard_map/dot_general | solution.py:36
  162.9 9.2 %all_gather.19 = bf16[1024,128]{1,0:T(8,128)(2,1)S(1)} all-gather(bf16[128,128]{1,0:T(8,128)(2,1)S(1)} %get-tuple-element.6), channel_id=1, replica_groups=mesh['outer'=4,'dev'=8] {'dev'}, dimensions={0}, use_global_device_ids=true | all-gather | bytes 294912 | tf_op jit(solution)/shard_map/all_gather | solution.py:45
  172.2 0.8 fusion.1
  173.0 1.0 copy.10
  (10 shorter events, 0.0 us)
Async XLA Ops:
  7.2 58.1 %copy-start = (bf16[1024,1024]{1,0:T(8,128)(2,1)S(1)}, bf16[1024,1024]{1,0:T(8,128)(2,1)}, u32[]{:S(2)}) copy-start(bf16[1024,1024]{1,0:T(8,128)(2,1)} %param.8) | copy-start | bytes 6291460
  7.2 58.1 %reduce-scatter.6.cloned.1.call-start = ((), (), s32[]{:S(2)}) async-start(), calls=%async_computation.4 | async-start | bytes 4718592 | tf_op jit(solution)/shard_map/reduce_scatter | solution.py:16
  11.2 93.1 %reduce-scatter.8.cloned.1.call-start = ((), (), s32[]{:S(2)}) async-start(), calls=%async_computation.5 | async-start | bytes 589824 | tf_op jit(solution)/shard_map/reduce_scatter | solution.py:19
  69.5 89.4 %reduce-scatter.4.cloned.1.call-start = ((), (), s32[]{:S(2)}) async-start(), calls=%async_computation.3 | async-start | bytes 4718592 | tf_op jit(solution)/shard_map/reduce_scatter | solution.py:27
  75.5 1.0 copy-start.2
  75.5 2.0 %copy-start.4 = (f32[128,128]{1,0:T(8,128)S(1)}, f32[128,128]{1,0:T(8,128)}, u32[]{:S(2)}) copy-start(f32[128,128]{1,0:T(8,128)} %param.10) | copy-start | bytes 196612
  75.5 11.8 %copy-start.5 = (f32[128,128]{1,0:T(8,128)S(1)}, f32[128,128]{1,0:T(8,128)}, u32[]{:S(2)}) copy-start(f32[128,128]{1,0:T(8,128)} %param.11) | copy-start | bytes 196612
  158.8 13.3 %copy-start.1 = (f32[1024,128]{0,1:T(8,128)S(1)}, f32[1024,128]{0,1:T(8,128)}, u32[]{:S(2)}) copy-start(f32[1024,128]{0,1:T(8,128)} %copy.9) | copy-start | bytes 1572868
  160.6 12.5 %copy-start.3 = (f32[128,128]{1,0:T(8,128)}, f32[128,128]{1,0:T(8,128)S(1)}, u32[]{:S(2)}) copy-start(f32[128,128]{1,0:T(8,128)S(1)} %fusion.3) | copy-start | bytes 196612
Sparse Core Ops, SparseCore 0:
  11.3 53.8 reduce-scatter.5
  69.6 34.6 reduce-scatter.7
  107.6 51.1 reduce-scatter.3
